TPU v7x, 1024 devices: a whole 4x4x32 slice. The times are simulated.
1024 devices in a mesh: dp: 64 (over z, core), cols: 16 (over y, x).
Axes of the slice: x: 4, y: 4, z: 32, core: 2. Of those that a mesh axis runs over, the one named last changes fastest.
Arguments:
- kv_latent: bfloat16 [8192, 512], P('dp', 'cols'), may hold values from -6 to 6
- kv_grad_out: bfloat16 [8192, 16384], P('dp'), may hold values from -8 to 8
- kv_weight: float32 [512, 16384], P('cols', 'dp'), may hold values from -6 to 6
- logit_max: float32 [64, 64], P('dp'), may hold values from 1 to 600, as said below
Outputs:
- kv_new: float32 [512, 16384], P('cols', 'dp')
Inputs may be any that keep to these rules, and one draw needn't show every extreme that they name: `logit_max`: each entry is a largest attention logit of one head over one index of dp's tokens.
All inputs are finite; a program needn't handle non-finite values.
Results may differ from a plain program's by a relative error of at most 0.0003.
Values sent between devices are 32-bit elements; how exact they have to be, the bound alone decides.
No kernel may reach another device: no remote copies, remote signals or barrier semaphores. Data moves between devices by JAX's collectives and lax.ppermute only.
A program may use at most 32 MiB of HBM per device.

v0:
```python
import math

import jax
import jax.numpy as jnp
from jax import lax
from jax.sharding import PartitionSpec as P

KR = 512
NOPE = 128
VD = 128
ITERS = 2
KD = 256


coef_first = 3.4445
coef_second = -4.775
coef_third = 2.0315
tau_logit = 100.0
learn_rate = 0.5
decay_rate = 0.1
highest = lax.Precision.HIGHEST


def gram_of(blocks):
    return jnp.einsum("hdr,her->hde", blocks, blocks, precision=highest)


def newton_step(current, gram):
    square = jnp.einsum("hde,hef->hdf", gram, gram, precision=highest)
    poly = coef_second * gram + coef_third * square
    return coef_first * current + jnp.einsum("hde,her->hdr", poly, current, precision=highest)


def scaled_start(blocks, gram):
    total = jnp.sum(jnp.diagonal(gram, axis1=1, axis2=2), axis=-1)
    factor = 1.0 / (jnp.sqrt(total) + 1e-07)
    return (blocks * factor[:, None, None], gram * (factor * factor)[:, None, None])


def group_newton(kv_blocks):
    kv_now = kv_blocks
    for step in range(ITERS):
        kv_gram = lax.psum(gram_of(kv_now), "cols")
        if step == 0:
            kv_now, kv_gram = scaled_start(kv_now, kv_gram)
        kv_now = newton_step(kv_now, kv_gram)
    return kv_now


def body(kv_latent, kv_grad_out, kv_weight, logit_max):
    head_count = kv_weight.shape[1] // KD
    kv_sum = lax.psum_scatter(
        lax.dot_general(
            kv_grad_out, kv_latent, (((0,), (0,)), ((), ())), preferred_element_type=jnp.float32
        ),
        "dp",
        scatter_dimension=0,
        tiled=True,
    )
    kv_blocks = kv_sum.reshape(head_count, KD, kv_sum.shape[1])
    kv_ortho = group_newton(kv_blocks)
    peak = lax.pmax(logit_max, "dp")
    owned = lax.dynamic_slice_in_dim(peak[0], lax.axis_index("dp") * head_count, head_count, 0)
    ratio = jnp.minimum(1.0, tau_logit / owned)
    root = jnp.sqrt(ratio)
    kv_factor = jnp.concatenate(
        [
            jnp.broadcast_to(root[:, None], (head_count, NOPE)),
            jnp.ones((head_count, VD), jnp.float32),
        ],
        axis=1,
    )
    columns = jnp.transpose(kv_ortho, (2, 0, 1)).reshape(kv_weight.shape)
    scale = 0.2 * math.sqrt(max(KR, KD))
    stepped = kv_weight - learn_rate * (scale * columns + decay_rate * kv_weight)
    return stepped * kv_factor


def solution(mesh):
    in_specs = (P("dp", "cols"), P("dp", None), P("cols", "dp"), P("dp", None))
    out_specs = P("cols", "dp")
    return jax.shard_map(body, mesh=mesh, in_specs=in_specs, out_specs=out_specs, check_vma=False)
```

profile of v0, /device:TPU:1, one launch (start us, length us, event | category | flops | bytes accessed | tf_op | source)
XLA Modules:
  0.0 562.8 jit_solution(3794918911153346856)
XLA Ops:
  6.5 0.0 copy-start
  6.5 0.0 reduce-scatter.2.cloned.1.call-start
  6.5 0.7 copy-done
  7.2 4.2 fusion.19
  11.5 0.0 copy-start.2
  11.5 0.0 copy-start.1
  11.5 0.0 reduce-scatter.2.cloned.1.call-update
  11.5 0.0 all-reduce.4.cloned.1.call-start
  11.5 219.9 %reduce-scatter.2.cloned.1.call-done = f32[256,32]{0,1:T(8,128)} async-done(((f32[16384,32]{0,1:T(8,128)}), f32[256,32]{0,1:T(8,128)}) %reduce-scatter.2.cloned.1.call-update) | async-done | bytes 32784 | tf_op jit(solution)/shard_map/reduce_scatter | solution.py:52
  231.5 1.9 convolution_bitcast_fusion.1
  233.4 0.0 all-reduce.4.cloned.1.call-update
  233.5 0.0 all-reduce.6.cloned.1.call-start
  233.5 155.8 %all-reduce.4.cloned.1.call-done = f32[1,256,256]{2,1,0:T(8,128)} async-done(((f32[1,256,256]{2,1,0:T(8,128)}), f32[1,256,256]{2,1,0:T(8,128)}) %all-reduce.4.cloned.1.call-update) | async-done | bytes 262160 | tf_op jit(solution)/shard_map/psum | solution.py:43
  389.3 2.6 gather_fusion
  391.9 0.6 reduce.1
  393.2 1.5 fusion.3
  394.7 1.2 convolution_add_fusion.1
  395.9 1.1 convolution_bitcast_fusion
  397.1 0.0 all-reduce.6.cloned.1.call-update
  397.1 0.0 copy-done.2
  397.1 95.2 %pmax.7 = f32[1,64]{1,0:T(1,128)S(1)} all-reduce(f32[1,64]{1,0:T(1,128)S(1)} %copy-done.2), channel_id=1, replica_groups=mesh['dp'=64,'cols'=16] {'dp'}, use_global_device_ids=true, to_apply=%region_4.5 | all-reduce | flops 64 | bytes 512 | tf_op jit(solution)/shard_map/pmax | solution.py:62
  492.3 0.6 fusion.18
  493.6 60.2 %all-reduce.6.cloned.1.call-done = f32[1,256,256]{2,1,0:T(8,128)} async-done(((f32[1,256,256]{2,1,0:T(8,128)}), f32[1,256,256]{2,1,0:T(8,128)}) %all-reduce.6.cloned.1.call-update) | async-done | bytes 262160 | tf_op jit(solution)/shard_map/psum | solution.py:43
  553.8 1.5 fusion.5
  555.3 0.0 copy-done.1
  555.3 1.0 fusion.11
  (3 shorter events, 0.0 us)
Async XLA Ops:
  6.5 0.7 copy-start
  6.5 224.9 %reduce-scatter.2.cloned.1.call-start = ((), (), s32[]{:S(2)}) async-start(), calls=%async_computation.1 | async-start | bytes 2129920 | tf_op jit(solution)/shard_map/reduce_scatter | solution.py:52
  11.5 385.6 %copy-start.2 = (f32[1,64]{1,0:T(1,128)S(1)}, f32[1,64]{1,0:T(1,128)}, u32[]{:S(2)}) copy-start(f32[1,64]{1,0:T(1,128)} %param.7) | copy-start | bytes 772
  11.5 543.8 %copy-start.1 = (f32[32,256]{1,0:T(8,128)S(1)}, f32[32,256]{1,0:T(8,128)}, u32[]{:S(2)}) copy-start(f32[32,256]{1,0:T(8,128)} %param.6) | copy-start | bytes 98308
  11.5 377.8 %all-reduce.4.cloned.1.call-start = ((), (), s32[]{:S(2)}) async-start(), calls=%async_computation.2 | async-start | bytes 524288 | tf_op jit(solution)/shard_map/psum | solution.py:43
  233.5 320.3 %all-reduce.6.cloned.1.call-start = ((), (), s32[]{:S(2)}) async-start(), calls=%async_computation.3 | async-start | bytes 524288 | tf_op jit(solution)/shard_map/psum | solution.py:43
Sparse Core Ops, SparseCore 0:
  11.6 219.8 reduce-scatter.1
  234.6 154.6 all-reduce.3
  397.2 156.5 all-reduce.5
where the time goes:
time: 564 us; the launch traced here: 563 us
  waiting for transfers between devices  436 us (77%)
  blocking collectives  95.2 us (17%)
  between operations  14.6 us (3%)
  matrix products  12.5 us (2%)
    reduce_scatter x1, waiting for transfers between devices, body(): lax.psum_scatter(lax.dot_general(kv_grad_out, kv_latent, (((0,), (0,)), (...  220 us
    psum x2, waiting for transfers between devices, group_newton(): kv_gram = lax.psum(gram_of(kv_now), 'cols')  216 us
    pmax x1, blocking collectives, body(): peak = lax.pmax(logit_max, 'dp')  95.2 us
  transfers between devices with their start and end apart: 3, of which 3 were waited for; matrix products, arithmetic and copies ran while one was open for 0% of the time, Pallas kernels for 0%

commit v1 on v0

v1 whole, which is shorter than its diff:
```python
import math

import jax
import jax.numpy as jnp
from jax import lax
from jax.experimental import pallas as pl
from jax.experimental.pallas import tpu as pltpu
from jax.sharding import PartitionSpec as P

KR = 512
NOPE = 128
KD = 256
HALF = 128
CORES = 2
NEAR = 4

coef_first = 3.4445
coef_second = -4.775
coef_third = 2.0315
tau_logit = 100.0
learn_rate = 0.5
decay_rate = 0.1
highest = lax.Precision.HIGHEST


def partial_kernel(parity_ref, latent_ref, grad_ref, logit_ref, out_ref, *, far, feats):
    step = pl.program_id(0)
    rows = 2 * feats
    for near in range(NEAR):
        start = pl.multiple_of((near * CORES + parity_ref[0]) * KD, KD)
        prod = jnp.dot(latent_ref[...], grad_ref[:, pl.ds(start, KD)], preferred_element_type=jnp.float32)
        for half in range(2):
            out_ref[near, pl.ds(step * rows + half * feats, feats), :] = prod[:, half * HALF : (half + 1) * HALF]

    @pl.when(step == 0)
    def _():
        heads = far * NEAR
        row = lax.broadcasted_iota(jnp.int32, (heads, heads * CORES), 0)
        lane = lax.broadcasted_iota(jnp.int32, (heads, heads * CORES), 1)
        owner = (row % far) * (NEAR * CORES) + (row // far) * CORES + parity_ref[0]
        spread = jnp.sum(jnp.where(lane == owner, logit_ref[...], 0.0), axis=1, keepdims=True)
        out_ref[:, far * rows :, :] = jnp.broadcast_to(spread, (heads, HALF)).reshape(NEAR, far, HALF)


def partial_sums(latent, grad, logit, parity, far):
    tokens, width = grad.shape
    feats = latent.shape[0]
    block = width // far
    depth = far * 2 * feats + far
    return pl.pallas_call(
        lambda *refs: partial_kernel(*refs, far=far, feats=feats),
        grid_spec=pltpu.PrefetchScalarGridSpec(
            num_scalar_prefetch=1,
            grid=(far,),
            in_specs=[
                pl.BlockSpec((feats, tokens), lambda i, _: (0, 0)),
                pl.BlockSpec((tokens, block), lambda i, _: (0, i)),
                pl.BlockSpec((1, logit.shape[1]), lambda i, _: (0, 0)),
            ],
            out_specs=pl.BlockSpec((NEAR, depth, HALF), lambda i, _: (0, 0, 0)),
        ),
        out_shape=jax.ShapeDtypeStruct((NEAR, depth, HALF), jnp.float32),
        name="partial_sums",
    )(parity, latent, grad, logit)


def near_kernel(in_ref, out_ref, *, far, rows):
    total = in_ref[0, : far * rows] + in_ref[1, : far * rows] + (in_ref[2, : far * rows] + in_ref[3, : far * rows])
    out_ref[:, :rows, :] = total.reshape(far, rows, HALF)
    tail = jnp.maximum(
        jnp.maximum(in_ref[0, far * rows :], in_ref[1, far * rows :]),
        jnp.maximum(in_ref[2, far * rows :], in_ref[3, far * rows :]),
    )
    out_ref[:, rows:, :] = jnp.broadcast_to(tail[:, None, :], (far, 8, HALF))


def in_vmem(count):
    return [pl.BlockSpec(memory_space=pltpu.VMEM)] * count


def near_sum(parts, far, rows):
    return pl.pallas_call(
        lambda *refs: near_kernel(*refs, far=far, rows=rows),
        in_specs=in_vmem(1),
        out_specs=in_vmem(1)[0],
        out_shape=jax.ShapeDtypeStruct((far, rows + 8, HALF), jnp.float32),
        name="near_sum",
    )(parts)


def far_kernel(in_ref, block_ref, peak_ref, *, rows):
    block_ref[...] = jnp.broadcast_to(jnp.sum(in_ref[:, :rows, :], axis=0), block_ref.shape)
    peak_ref[...] = jnp.max(in_ref[:, rows:, :], axis=0)


def far_sum(parts, rows, copies):
    return pl.pallas_call(
        lambda *refs: far_kernel(*refs, rows=rows),
        in_specs=in_vmem(1),
        out_specs=tuple(in_vmem(2)),
        out_shape=(
            jax.ShapeDtypeStruct((copies, rows, HALF), jnp.float32),
            jax.ShapeDtypeStruct((8, HALF), jnp.float32),
        ),
        name="far_sum",
    )(parts)


def final_kernel(all_ref, own_ref, peak_ref, weight_ref, out_ref, *, feats):
    def mul(left, right):
        return jnp.dot(left, right, precision=highest, preferred_element_type=jnp.float32)

    count = all_ref.shape[0]
    whole = jnp.concatenate(
        [
            all_ref[:, :feats, :].reshape(count * feats, HALF),
            all_ref[:, feats:, :].reshape(count * feats, HALF),
        ],
        axis=1,
    )
    gram = lax.dot_general(
        whole, whole, (((0,), (0,)), ((), ())), precision=highest, preferred_element_type=jnp.float32
    )
    total = jnp.sum(whole * whole)
    row = lax.broadcasted_iota(jnp.int32, (KD, KD), 0)
    col = lax.broadcasted_iota(jnp.int32, (KD, KD), 1)
    eye = jnp.where(row == col, coef_first, 0.0)
    factor = 1.0 / (jnp.sqrt(jnp.broadcast_to(total, (1, KD))) + 1e-07)
    first = gram * (factor * factor)
    poly_first = eye + coef_second * first + coef_third * mul(first, first)
    second = mul(mul(poly_first, first), poly_first)
    poly_second = eye + coef_second * second + coef_third * mul(second, second)
    own = jnp.concatenate([own_ref[0, :feats, :], own_ref[0, feats:, :]], axis=1) * factor
    ortho = mul(mul(own, poly_first), poly_second)
    scale = 0.2 * math.sqrt(max(KR, KD))
    weight = weight_ref[...]
    stepped = weight - learn_rate * (scale * ortho + decay_rate * weight)
    root = jnp.sqrt(jnp.minimum(1.0, tau_logit / peak_ref[:1, :]))
    clip = jnp.concatenate([root, jnp.ones((1, KD - NOPE), jnp.float32)], axis=1)
    out_ref[...] = stepped * clip


def finish(blocks, own, peak, weight):
    return pl.pallas_call(
        lambda *refs: final_kernel(*refs, feats=weight.shape[0]),
        in_specs=in_vmem(4),
        out_specs=in_vmem(1)[0],
        out_shape=jax.ShapeDtypeStruct(weight.shape, jnp.float32),
        name="finish",
    )(blocks, own, peak, weight)


def stage_groups(size):
    chips = size // CORES
    near = []
    for core in range(CORES):
        for window in range(chips // NEAR):
            members = [(NEAR * window + core * (NEAR // 2) + k) % chips for k in range(NEAR)]
            near.append([CORES * z + core for z in sorted(members, key=lambda z: z % NEAR)])
    far = [
        [CORES * z + core for z in range(kind, chips, NEAR)] for kind in range(NEAR) for core in range(CORES)
    ]
    return near, far


def body(kv_latent, kv_grad_out, kv_weight, logit_max, size, cols):
    far = size // (NEAR * CORES)
    feats = kv_latent.shape[1]
    rows = 2 * feats
    near, distant = stage_groups(size)

    def exchange(value, groups):
        return lax.all_to_all(value, "dp", 0, 0, axis_index_groups=groups, tiled=True)

    latent = kv_latent.T
    parity = (lax.axis_index("dp") % CORES).reshape(1)
    sent = partial_sums(latent, kv_grad_out, logit_max, 1 - parity, far)
    taken = lax.ppermute(sent, "dp", [(i, i ^ 1) for i in range(size)])
    kept = partial_sums(latent, kv_grad_out, logit_max, parity, far)
    is_sum = lax.broadcasted_iota(jnp.int32, kept.shape, 1) < far * rows
    parts = jnp.where(is_sum, kept + taken, jnp.maximum(kept, taken))
    parts = exchange(parts, near)
    parts = exchange(near_sum(parts, far, rows), distant)
    copies, peak = far_sum(parts, rows, cols)
    blocks = lax.all_to_all(copies, "cols", 0, 0, tiled=True)
    return finish(blocks, copies, peak, kv_weight)


def solution(mesh):
    in_specs = (P("dp", "cols"), P("dp", None), P("cols", "dp"), P("dp", None))
    out_specs = P("cols", "dp")
    size, cols = mesh.shape["dp"], mesh.shape["cols"]
    return jax.shard_map(
        lambda *args: body(*args, size, cols), mesh=mesh, in_specs=in_specs, out_specs=out_specs, check_vma=False
    )
```

time: 564 us -> 140 us (0.25)
  the two profiles are of different devices: /device:TPU:1 before, /device:TPU:64 now
where the time goes in v1:
time: 140 us; the launch traced here: 139 us
  blocking collectives  114 us (81%)
  Pallas kernels  21.3 us (15%)
  starting transfers between devices  1.91 us (1%)
  other arithmetic  1.66 us (1%)
    all_to_all x2, blocking collectives, exchange(): lax.all_to_all(value, 'dp', 0, 0, axis_index_groups=groups, tiled=True)  96.1 us
    all_to_all x1, blocking collectives, body(): blocks = lax.all_to_all(copies, 'cols', 0, 0, tiled=True)  18.2 us
    pallas_call x2, Pallas kernels, partial_sums(): pl.pallas_call(lambda *refs: partial_kernel(*refs, far=far, feats=feats),...  12.4 us
    pallas_call x1, Pallas kernels, finish(): pl.pallas_call(lambda *refs: final_kernel(*refs, feats=weight.shape[0]),...  5.11 us
  transfers between devices with their start and end apart: 1, of which 0 were waited for; matrix products, arithmetic and copies ran while one was open for 0% of the time, Pallas kernels for 4%

profile of v1, /device:TPU:64, one launch (start us, length us, event | category | flops | bytes accessed | tf_op | source)
XLA Modules:
  0.0 139.2 jit_solution(4798606195720825466)
XLA Ops:
  0.0 6.2 %partial_sums.3 = f32[4,520,128]{2,1,0:T(8,128)} custom-call(s32[1]{0:T(128)S(6)} %sub.3.refs_0_, bf16[32,128]{1,0:T(8,128)(2,1)} %bitcast.2, bf16[128,16384]{1,0:T(8,128)(2,1)} %refs_2_.3, f32[1,64]{1,0:T(1,128)} %refs_3_.4), custom_call_target="tpu_custom_call" | custom-call | tf_op jit(solution)/shard_map/partial_sums/pallas_call | solution.py:50
  6.2 1.9 %collective-permute-start = (f32[4,520,128]{2,1,0:T(8,128)}, f32[4,520,128]{2,1,0:T(8,128)S(1)}, u32[]{:S(2)}, u32[]{:S(2)}) collective-permute-start(f32[4,520,128]{2,1,0:T(8,128)} %partial_sums.3), channel_id=1, source_target_pairs={{0,16},{16,0},{32,48},{48,32},{64,80},{80,64},{96,112},{112,96},{1... | collective-permute-start | bytes 3194888 | tf_op jit(solution)/shard_map/ppermute | solution.py:178
  8.1 6.2 %partial_sums.2 = f32[4,520,128]{2,1,0:T(8,128)} custom-call(s32[1]{0:T(128)} %bitcast.refs_0_, bf16[32,128]{1,0:T(8,128)(2,1)} %bitcast.3, bf16[128,16384]{1,0:T(8,128)(2,1)} %refs_2_.3, f32[1,64]{1,0:T(1,128)} %refs_3_.4), custom_call_target="tpu_custom_call" | custom-call | tf_op jit(solution)/shard_map/partial_sums/pallas_call | solution.py:50
  14.3 0.0 collective-permute-done
  14.3 1.7 %maximum_select_fusion = f32[4,520,128]{2,1,0:T(8,128)S(1)} fusion(f32[4,520,128]{2,1,0:T(8,128)} %partial_sums.2, f32[4,520,128]{2,1,0:T(8,128)S(1)} %collective-permute-done, pred[520]{0:T(1024)(128)(4,1)S(1)} %iota_compare_fusion), kind=kLoop, calls=%fused_computation | loop fusion | flops 798720 | bytes 3195400 | tf_op jit(solution)/shard_map/jit(_where)/select_n | solution.py:181
  16.0 32.5 %all_to_all.15.refs_0_ = f32[4,520,128]{2,1,0:T(8,128)} all-to-all(f32[4,520,128]{2,1,0:T(8,128)S(1)} %maximum_select_fusion), channel_id=1, replica_groups={{0,32,64,96},{128,160,192,224},{256,288,320,352},{384,416,448,480},{512..., dimensions={0} | all-to-all | bytes 2129920 | tf_op jit(solution)/shard_map/all_to_all | solution.py:173
  48.5 2.0 %near_sum.1 = f32[8,72,128]{2,1,0:T(8,128)} custom-call(f32[4,520,128]{2,1,0:T(8,128)} %all_to_all.15.refs_0_), custom_call_target="tpu_custom_call" | custom-call | tf_op jit(solution)/shard_map/near_sum/pallas_call | solution.py:82
  50.4 63.6 %all_to_all.16.refs_0_ = f32[8,72,128]{2,1,0:T(8,128)} all-to-all(f32[8,72,128]{2,1,0:T(8,128)} %near_sum.1), channel_id=1, replica_groups={{0,128,256,384,512,640,768,896},{16,144,272,400,528,656,784,912},{32,16..., dimensions={0} | all-to-all | bytes 589824 | tf_op jit(solution)/shard_map/all_to_all | solution.py:173
  114.1 1.8 %far_sum.1 = (f32[16,64,128]{2,1,0:T(8,128)}, f32[8,128]{1,0:T(8,128)}) custom-call(f32[8,72,128]{2,1,0:T(8,128)} %all_to_all.16.refs_0_), custom_call_target="tpu_custom_call" | custom-call | tf_op jit(solution)/shard_map/far_sum/pallas_call | solution.py:97
  115.9 18.2 %all_to_all.17.refs_0_ = f32[16,64,128]{2,1,0:T(8,128)} all-to-all(f32[16,64,128]{2,1,0:T(8,128)} %get-tuple-element.7.refs_1_), channel_id=1, replica_groups=mesh['dp'=64,'cols'=16] {'cols'}, dimensions={0} | all-to-all | bytes 1048576 | tf_op jit(solution)/shard_map/all_to_all | solution.py:185
  134.1 5.1 %finish.1 = f32[32,256]{1,0:T(8,128)} custom-call(f32[16,64,128]{2,1,0:T(8,128)} %all_to_all.17.refs_0_, f32[16,64,128]{2,1,0:T(8,128)} %get-tuple-element.7.refs_1_, f32[8,128]{1,0:T(8,128)} %get-tuple-element.8.refs_2_, f32[32,256]{1,0:T(8,128)} %refs_3_.5), custom_call_target="tpu_custom_call" | custom-call | tf_op jit(solution)/shard_map/finish/pallas_call | solution.py:144
  (1 shorter events, 0.0 us)
Async XLA Ops:
  6.2 8.1 %collective-permute-start = (f32[4,520,128]{2,1,0:T(8,128)}, f32[4,520,128]{2,1,0:T(8,128)S(1)}, u32[]{:S(2)}, u32[]{:S(2)}) collective-permute-start(f32[4,520,128]{2,1,0:T(8,128)} %partial_sums.3), channel_id=1, source_target_pairs={{0,16},{16,0},{32,48},{48,32},{64,80},{80,64},{96,112},{112,96},{1... | collective-permute-start | bytes 3194888 | tf_op jit(solution)/shard_map/ppermute | solution.py:178

commit v2 on v1

v2 whole, which is shorter than its diff:
```python
import functools
import math

import jax
import jax.numpy as jnp
from jax import lax
from jax.experimental import pallas as pl
from jax.experimental.pallas import tpu as pltpu
from jax.sharding import PartitionSpec as P

KR = 512
NOPE = 128
KD = 256
HALF = 128
CORES = 2
NEAR = 4
GROUPS = 2

coef_first = 3.4445
coef_second = -4.775
coef_third = 2.0315
tau_logit = 100.0
learn_rate = 0.5
decay_rate = 0.1


def in_vmem(value):
    return pltpu.with_memory_space_constraint(value, pltpu.VMEM)


def partial_kernel(parity_ref, latent_ref, grad_ref, logit_ref, out_ref, buffer, sems, *, far, feats):
    rows = 2 * feats
    heads = far * NEAR
    copies = []
    for head in range(heads):
        start = pl.multiple_of((head * CORES + parity_ref[0]) * KD, KD)
        copies.append(
            pltpu.make_async_copy(
                grad_ref.at[:, pl.ds(start, KD)], buffer.at[:, head * KD : (head + 1) * KD], sems.at[head]
            )
        )
    for copy in copies:
        copy.start()

    row = lax.broadcasted_iota(jnp.int32, (heads, heads * CORES), 0)
    lane = lax.broadcasted_iota(jnp.int32, (heads, heads * CORES), 1)
    owner = (row % far) * (NEAR * CORES) + (row // far) * CORES + parity_ref[0]
    spread = jnp.sum(jnp.where(lane == owner, logit_ref[...], 0.0), axis=1, keepdims=True)
    out_ref[:, far * rows :, :] = jnp.broadcast_to(spread, (heads, HALF)).reshape(NEAR, far, HALF)

    batch = heads // GROUPS
    for group in range(GROUPS):
        members = range(group * batch, (group + 1) * batch)
        for head in members:
            copies[head].wait()
        block = buffer[:, group * batch * KD : (group + 1) * batch * KD]
        prod = jnp.dot(latent_ref[...], block, preferred_element_type=jnp.float32)
        for head in members:
            distant, near = head // NEAR, head % NEAR
            for half in range(2):
                low = (head - group * batch) * KD + half * HALF
                first = distant * rows + half * feats
                out_ref[near, first : first + feats, :] = prod[:, low : low + HALF]


def partial_sums(latent, grad, logit, parity, far):
    feats = latent.shape[0]
    tokens, width = grad.shape
    depth = far * 2 * feats + far
    return pl.pallas_call(
        functools.partial(partial_kernel, far=far, feats=feats),
        in_specs=[
            pl.BlockSpec(memory_space=pltpu.SMEM),
            pl.BlockSpec(memory_space=pltpu.VMEM),
            pl.BlockSpec(memory_space=pl.ANY),
            pl.BlockSpec(memory_space=pltpu.VMEM),
        ],
        out_shape=pltpu.VMEM((NEAR, depth, HALF), jnp.float32),
        scratch_shapes=[
            pltpu.VMEM((tokens, width // CORES), jnp.bfloat16),
            pltpu.SemaphoreType.DMA((far * NEAR,)),
        ],
        name="partial_sums",
    )(parity, latent, grad, logit)


def near_kernel(in_ref, out_ref, *, far, rows):
    depth = far * rows
    for distant in range(far):
        low, high = distant * rows, (distant + 1) * rows
        base = distant * (rows + 1)
        out_ref[base : base + rows, :] = (in_ref[0, low:high] + in_ref[1, low:high]) + (
            in_ref[2, low:high] + in_ref[3, low:high]
        )
    tail = jnp.maximum(
        jnp.maximum(in_ref[0, depth:], in_ref[1, depth:]), jnp.maximum(in_ref[2, depth:], in_ref[3, depth:])
    )
    for distant in range(far):
        base = distant * (rows + 1) + rows
        out_ref[base : base + 1, :] = tail[distant : distant + 1]


def near_sum(parts, far, rows):
    return pl.pallas_call(
        functools.partial(near_kernel, far=far, rows=rows),
        out_shape=pltpu.VMEM((far * (rows + 1), HALF), jnp.float32),
        name="near_sum",
    )(in_vmem(parts))


def far_kernel(in_ref, block_ref, peak_ref, *, far, rows):
    sums = [in_ref[k * (rows + 1) : k * (rows + 1) + rows, :] for k in range(far)]
    peaks = [in_ref[k * (rows + 1) + rows : (k + 1) * (rows + 1), :] for k in range(far)]
    block_ref[...] = jnp.broadcast_to(functools.reduce(jnp.add, sums), block_ref.shape)
    peak_ref[...] = jnp.broadcast_to(functools.reduce(jnp.maximum, peaks), peak_ref.shape)


def far_sum(parts, far, rows, copies):
    return pl.pallas_call(
        functools.partial(far_kernel, far=far, rows=rows),
        out_shape=(pltpu.VMEM((copies, rows, HALF), jnp.float32), pltpu.VMEM((8, HALF), jnp.float32)),
        name="far_sum",
    )(in_vmem(parts))


def parted(value):
    high = value.astype(jnp.bfloat16)
    return high, (value - high.astype(jnp.float32)).astype(jnp.bfloat16)


def single(left, right, dims=(((1,), (0,)), ((), ()))):
    return lax.dot_general(left, right, dims, preferred_element_type=jnp.float32)


def product(left, right):
    return single(left[0], right[0]) + (single(left[0], right[1]) + single(left[1], right[0]))


def final_kernel(all_ref, own_ref, peak_ref, weight_ref, out_ref, *, feats):
    count = all_ref.shape[0]
    whole = jnp.concatenate(
        [
            all_ref[:, :feats, :].reshape(count * feats, HALF),
            all_ref[:, feats:, :].reshape(count * feats, HALF),
        ],
        axis=1,
    )
    high, low = parted(whole)
    over_rows = (((0,), (0,)), ((), ()))
    mixed = single(high, low, over_rows)
    gram = single(high, high, over_rows) + (mixed + mixed.T)
    total = jnp.sum(whole * whole)
    factor = 1.0 / (jnp.sqrt(jnp.broadcast_to(total, (1, KD))) + 1e-07)
    row = lax.broadcasted_iota(jnp.int32, (KD, KD), 0)
    col = lax.broadcasted_iota(jnp.int32, (KD, KD), 1)
    first = gram * (factor * factor)
    split_first = parted(first)
    poly = jnp.where(row == col, coef_first, 0.0) + coef_second * first + coef_third * product(split_first, split_first)
    split_poly = parted(poly)
    own = jnp.concatenate([own_ref[0, :feats, :], own_ref[0, feats:, :]], axis=1) * factor
    current = product(parted(own), split_poly)
    second = parted(product(parted(product(split_poly, split_first)), split_poly))
    once = product(parted(current), second)
    twice = product(parted(once), second)
    ortho = coef_first * current + coef_second * once + coef_third * twice
    scale = 0.2 * math.sqrt(max(KR, KD))
    weight = weight_ref[...]
    stepped = weight - learn_rate * (scale * ortho + decay_rate * weight)
    root = jnp.sqrt(jnp.minimum(1.0, tau_logit / peak_ref[:1, :]))
    clip = jnp.concatenate([root, jnp.ones((1, KD - NOPE), jnp.float32)], axis=1)
    out_ref[...] = stepped * clip


def finish(blocks, own, peak, weight):
    return pl.pallas_call(
        functools.partial(final_kernel, feats=weight.shape[0]),
        out_shape=jax.ShapeDtypeStruct(weight.shape, jnp.float32),
        name="finish",
    )(in_vmem(blocks), in_vmem(own), in_vmem(peak), in_vmem(weight))


def stage_groups(size):
    chips = size // CORES
    near = []
    for core in range(CORES):
        for window in range(chips // NEAR):
            members = [(NEAR * window + core * (NEAR // 2) + k) % chips for k in range(NEAR)]
            near.append([CORES * z + core for z in sorted(members, key=lambda z: z % NEAR)])
    far = [
        [CORES * z + core for z in range(kind, chips, NEAR)] for kind in range(NEAR) for core in range(CORES)
    ]
    return near, far


def body(kv_latent, kv_grad_out, kv_weight, logit_max, size, cols):
    far = size // (NEAR * CORES)
    feats = kv_latent.shape[1]
    rows = 2 * feats
    near, distant = stage_groups(size)

    def exchange(value, groups):
        return lax.all_to_all(value, "dp", 0, 0, axis_index_groups=groups, tiled=True)

    latent = kv_latent.T
    parity = (lax.axis_index("dp") % CORES).reshape(1)
    sent = partial_sums(latent, kv_grad_out, logit_max, 1 - parity, far)
    taken = lax.ppermute(sent, "dp", [(i, i ^ 1) for i in range(size)])
    kept = partial_sums(latent, kv_grad_out, logit_max, parity, far)
    is_sum = lax.broadcasted_iota(jnp.int32, kept.shape, 1) < far * rows
    parts = jnp.where(is_sum, kept + taken, jnp.maximum(kept, taken))
    summed = near_sum(exchange(parts, near), far, rows)
    parts = exchange(summed.reshape(far, 1, -1), distant).reshape(summed.shape)
    copies, peak = far_sum(parts, far, rows, cols)
    blocks = lax.all_to_all(copies, "cols", 0, 0, tiled=True)
    return finish(blocks, copies, peak, kv_weight)


def solution(mesh):
    in_specs = (P("dp", "cols"), P("dp", None), P("cols", "dp"), P("dp", None))
    out_specs = P("cols", "dp")
    size, cols = mesh.shape["dp"], mesh.shape["cols"]
    return jax.shard_map(
        lambda *args: body(*args, size, cols), mesh=mesh, in_specs=in_specs, out_specs=out_specs, check_vma=False
    )
```

time: 140 us -> 122 us (0.87)
  Pallas kernels: 21.3 us -> 8.2 us
  blocking collectives: 114 us -> 111 us
    pallas_call x5, Pallas kernels: 21.3 us -> 8.2 us  [the longest x2 5.7 us: partial_sums(): pl.pallas_call(functools.partial(partial_kernel, far=far, feats=feats), i...]
    all_to_all x2, blocking collectives: 96.1 us -> 93 us  [exchange(): lax.all_to_all(value, 'dp', 0, 0, axis_index_groups=groups, tiled=True)]
  transfers between devices with their start and end apart: 1 -> 1, of which waited for: 0 -> 0; matrix products, arithmetic and copies ran while one was open for 0% -> 0% of each run, Pallas kernels for 4% -> 2%
where the time goes in v2:
time: 122 us
  blocking collectives  111 us (91%)
  Pallas kernels  8.2 us (7%)
  starting transfers between devices  1.92 us (2%)
    all_to_all x2, blocking collectives, exchange(): lax.all_to_all(value, 'dp', 0, 0, axis_index_groups=groups, tiled=True)  93 us
    all_to_all x1, blocking collectives, body(): blocks = lax.all_to_all(copies, 'cols', 0, 0, tiled=True)  18 us
    pallas_call x2, Pallas kernels, partial_sums(): pl.pallas_call(functools.partial(partial_kernel, far=far, feats=feats), i...  5.7 us
  transfers between devices with their start and end apart: 1, of which 0 were waited for; matrix products, arithmetic and copies ran while one was open for 0% of the time, Pallas kernels for 2%

profile of v2, /device:TPU:64, one launch (start us, length us, event | category | flops | bytes accessed | tf_op | source)
XLA Modules:
  0.0 121.7 jit_solution(7488567269625454289)
XLA Ops:
  0.0 2.8 %partial_sums.3 = f32[4,520,128]{2,1,0:T(8,128)S(1)} custom-call(s32[1]{0:T(128)S(6)} %sub.3.parity_ref, bf16[32,128]{1,0:T(8,128)(2,1)} %bitcast.6, bf16[128,16384]{1,0:T(8,128)(2,1)} %grad_ref.3, f32[1,64]{1,0:T(1,128)} %logit_ref.3), custom_call_target="tpu_custom_call" | custom-call | tf_op jit(solution)/shard_map/partial_sums/pallas_call | solution.py:70
  2.9 1.9 %collective-permute-start = (f32[4,520,128]{2,1,0:T(8,128)S(1)}, f32[4,520,128]{2,1,0:T(8,128)S(1)}, u32[]{:S(2)}, u32[]{:S(2)}) collective-permute-start(f32[4,520,128]{2,1,0:T(8,128)S(1)} %partial_sums.3), channel_id=1, source_target_pairs={{0,16},{16,0},{32,48},{48,32},{64,80},{80,64},{96,112},{112,96},{1... | collective-permute-start | bytes 3194888 | tf_op jit(solution)/shard_map/ppermute | solution.py:207
  4.8 2.8 %partial_sums.2 = f32[4,520,128]{2,1,0:T(8,128)S(1)} custom-call(s32[1]{0:T(128)} %bitcast.parity_ref, bf16[32,128]{1,0:T(8,128)(2,1)} %bitcast.7, bf16[128,16384]{1,0:T(8,128)(2,1)} %grad_ref.3, f32[1,64]{1,0:T(1,128)} %logit_ref.3), custom_call_target="tpu_custom_call" | custom-call | tf_op jit(solution)/shard_map/partial_sums/pallas_call | solution.py:70
  7.7 0.0 collective-permute-done
  7.7 0.5 maximum_select_fusion
  8.2 31.5 %all_to_all.15.in_ref = f32[4,520,128]{2,1,0:T(8,128)S(1)} all-to-all(f32[4,520,128]{2,1,0:T(8,128)S(1)} %maximum_select_fusion), channel_id=1, replica_groups={{0,32,64,96},{128,160,192,224},{256,288,320,352},{384,416,448,480},{512..., dimensions={0} | all-to-all | bytes 2129920 | tf_op jit(solution)/shard_map/all_to_all | solution.py:202
  39.8 0.0 copy-start
  39.8 61.5 %all_to_all.16 = f32[8,1,8320]{2,1,0:T(1,128)S(1)} all-to-all(f32[8,1,8320]{2,1,0:T(1,128)S(1)} %bitcast.5), channel_id=1, replica_groups={{0,128,256,384,512,640,768,896},{16,144,272,400,528,656,784,912},{32,16..., dimensions={0} | all-to-all | bytes 532480 | tf_op jit(solution)/shard_map/all_to_all | solution.py:202
  101.3 0.1 far_sum.1
  101.4 18.0 %all_to_all.17.all_ref = f32[16,64,128]{2,1,0:T(8,128)S(1)} all-to-all(f32[16,64,128]{2,1,0:T(8,128)S(1)} %get-tuple-element.7.own_ref), channel_id=1, replica_groups=mesh['dp'=64,'cols'=16] {'cols'}, dimensions={0} | all-to-all | bytes 1048576 | tf_op jit(solution)/shard_map/all_to_all | solution.py:214
  119.3 0.0 copy-done
  119.3 2.4 %finish.1 = f32[32,256]{1,0:T(8,128)} custom-call(f32[16,64,128]{2,1,0:T(8,128)S(1)} %all_to_all.17.all_ref, f32[16,64,128]{2,1,0:T(8,128)S(1)} %get-tuple-element.7.own_ref, f32[8,128]{1,0:T(8,128)S(1)} %get-tuple-element.8.peak_ref, f32[32,256]{1,0:T(8,128)S(1)} %copy-done), custom_call_target="tpu_custom_call" | custom-call | tf_op jit(solution)/shard_map/finish/pallas_call | solution.py:175
  (2 shorter events, 0.1 us)
Async XLA Ops:
  2.9 4.8 %collective-permute-start = (f32[4,520,128]{2,1,0:T(8,128)S(1)}, f32[4,520,128]{2,1,0:T(8,128)S(1)}, u32[]{:S(2)}, u32[]{:S(2)}) collective-permute-start(f32[4,520,128]{2,1,0:T(8,128)S(1)} %partial_sums.3), channel_id=1, source_target_pairs={{0,16},{16,0},{32,48},{48,32},{64,80},{80,64},{96,112},{112,96},{1... | collective-permute-start | bytes 3194888 | tf_op jit(solution)/shard_map/ppermute | solution.py:207
  39.8 79.6 %copy-start = (f32[32,256]{1,0:T(8,128)S(1)}, f32[32,256]{1,0:T(8,128)}, u32[]{:S(2)}) copy-start(f32[32,256]{1,0:T(8,128)} %weight_ref.1) | copy-start | bytes 98308

commit v3 on v2

--- a/solution.py
+++ b/solution.py
@@ -15,6 +15,9 @@
 CORES = 2
 NEAR = 4
 GROUPS = 2
+FAR_ORDER = (3, 2, 1, 0, 7, 6, 5, 4)
+NEAR_ORDER = (3, 2, 1, 0)
+COL_ORDER = (15, 14, 13, 12, 11, 10, 9, 8, 7, 6, 5, 4, 3, 2, 1, 0)
 
 coef_first = 3.4445
 coef_second = -4.775
@@ -28,12 +31,21 @@
     return pltpu.with_memory_space_constraint(value, pltpu.VMEM)
 
 
-def partial_kernel(parity_ref, latent_ref, grad_ref, logit_ref, out_ref, buffer, sems, *, far, feats):
+def partial_kernel(latent_hbm, grad_ref, logit_hbm, out_ref, latent_ref, logit_ref, buffer, sems, *, far, feats, other):
     rows = 2 * feats
     heads = far * NEAR
+    parity = lax.axis_index("dp") % CORES
+    if other:
+        parity = 1 - parity
+    side = [
+        pltpu.make_async_copy(logit_hbm, logit_ref, sems.at[heads]),
+        pltpu.make_async_copy(latent_hbm, latent_ref, sems.at[heads + 1]),
+    ]
+    for copy in side:
+        copy.start()
     copies = []
     for head in range(heads):
-        start = pl.multiple_of((head * CORES + parity_ref[0]) * KD, KD)
+        start = pl.multiple_of((head * CORES + parity) * KD, KD)
         copies.append(
             pltpu.make_async_copy(
                 grad_ref.at[:, pl.ds(start, KD)], buffer.at[:, head * KD : (head + 1) * KD], sems.at[head]
@@ -42,9 +54,13 @@
     for copy in copies:
         copy.start()
 
+    for copy in side:
+        copy.wait()
     row = lax.broadcasted_iota(jnp.int32, (heads, heads * CORES), 0)
     lane = lax.broadcasted_iota(jnp.int32, (heads, heads * CORES), 1)
-    owner = (row % far) * (NEAR * CORES) + (row // far) * CORES + parity_ref[0]
+    slot = row // far
+    kind = sum(jnp.where(slot == k, NEAR_ORDER[k], 0) for k in range(NEAR))
+    owner = (row % far) * (NEAR * CORES) + kind * CORES + parity
     spread = jnp.sum(jnp.where(lane == owner, logit_ref[...], 0.0), axis=1, keepdims=True)
     out_ref[:, far * rows :, :] = jnp.broadcast_to(spread, (heads, HALF)).reshape(NEAR, far, HALF)
 
@@ -60,35 +76,32 @@
             for half in range(2):
                 low = (head - group * batch) * KD + half * HALF
                 first = distant * rows + half * feats
-                out_ref[near, first : first + feats, :] = prod[:, low : low + HALF]
-
-
-def partial_sums(latent, grad, logit, parity, far):
+                out_ref[NEAR_ORDER.index(near), first : first + feats, :] = prod[:, low : low + HALF]
+
+
+def partial_sums(latent, grad, logit, far, other):
     feats = latent.shape[0]
     tokens, width = grad.shape
     depth = far * 2 * feats + far
     return pl.pallas_call(
-        functools.partial(partial_kernel, far=far, feats=feats),
-        in_specs=[
-            pl.BlockSpec(memory_space=pltpu.SMEM),
-            pl.BlockSpec(memory_space=pltpu.VMEM),
-            pl.BlockSpec(memory_space=pl.ANY),
-            pl.BlockSpec(memory_space=pltpu.VMEM),
-        ],
+        functools.partial(partial_kernel, far=far, feats=feats, other=other),
+        in_specs=[pl.BlockSpec(memory_space=pl.ANY)] * 3,
         out_shape=pltpu.VMEM((NEAR, depth, HALF), jnp.float32),
         scratch_shapes=[
-            pltpu.VMEM((tokens, width // CORES), jnp.bfloat16),
-            pltpu.SemaphoreType.DMA((far * NEAR,)),
+            pltpu.VMEM(latent.shape, latent.dtype),
+            pltpu.VMEM(logit.shape, logit.dtype),
+            pltpu.VMEM((tokens, width // CORES), grad.dtype),
+            pltpu.SemaphoreType.DMA((far * NEAR + 2,)),
         ],
-        name="partial_sums",
-    )(parity, latent, grad, logit)
+        name="partial_other" if other else "partial_own",
+    )(latent, grad, logit)
 
 
 def near_kernel(in_ref, out_ref, *, far, rows):
     depth = far * rows
     for distant in range(far):
         low, high = distant * rows, (distant + 1) * rows
-        base = distant * (rows + 1)
+        base = FAR_ORDER.index(distant) * (rows + 1)
         out_ref[base : base + rows, :] = (in_ref[0, low:high] + in_ref[1, low:high]) + (
             in_ref[2, low:high] + in_ref[3, low:high]
         )
@@ -96,7 +109,7 @@
         jnp.maximum(in_ref[0, depth:], in_ref[1, depth:]), jnp.maximum(in_ref[2, depth:], in_ref[3, depth:])
     )
     for distant in range(far):
-        base = distant * (rows + 1) + rows
+        base = FAR_ORDER.index(distant) * (rows + 1) + rows
         out_ref[base : base + 1, :] = tail[distant : distant + 1]
 
 
@@ -185,9 +198,9 @@
     for core in range(CORES):
         for window in range(chips // NEAR):
             members = [(NEAR * window + core * (NEAR // 2) + k) % chips for k in range(NEAR)]
-            near.append([CORES * z + core for z in sorted(members, key=lambda z: z % NEAR)])
+            near.append([CORES * z + core for z in sorted(members, key=lambda z: NEAR_ORDER.index(z % NEAR))])
     far = [
-        [CORES * z + core for z in range(kind, chips, NEAR)] for kind in range(NEAR) for core in range(CORES)
+        [CORES * (kind + NEAR * k) + core for k in FAR_ORDER] for kind in range(NEAR) for core in range(CORES)
     ]
     return near, far
 
@@ -202,16 +215,15 @@
         return lax.all_to_all(value, "dp", 0, 0, axis_index_groups=groups, tiled=True)
 
     latent = kv_latent.T
-    parity = (lax.axis_index("dp") % CORES).reshape(1)
-    sent = partial_sums(latent, kv_grad_out, logit_max, 1 - parity, far)
+    sent = partial_sums(latent, kv_grad_out, logit_max, far, True)
     taken = lax.ppermute(sent, "dp", [(i, i ^ 1) for i in range(size)])
-    kept = partial_sums(latent, kv_grad_out, logit_max, parity, far)
+    kept = partial_sums(latent, kv_grad_out, logit_max, far, False)
     is_sum = lax.broadcasted_iota(jnp.int32, kept.shape, 1) < far * rows
     parts = jnp.where(is_sum, kept + taken, jnp.maximum(kept, taken))
     summed = near_sum(exchange(parts, near), far, rows)
     parts = exchange(summed.reshape(far, 1, -1), distant).reshape(summed.shape)
     copies, peak = far_sum(parts, far, rows, cols)
-    blocks = lax.all_to_all(copies, "cols", 0, 0, tiled=True)
+    blocks = lax.all_to_all(copies, "cols", 0, 0, axis_index_groups=[list(COL_ORDER)], tiled=True)
     return finish(blocks, copies, peak, kv_weight)
 
 

time: 122 us -> 109 us (0.89)
  the two profiles are of different devices: /device:TPU:64 before, /device:TPU:1 now
where the time goes in v3:
time: 109 us
  blocking collectives  85.2 us (78%)
  starting transfers between devices  16 us (15%)
  Pallas kernels  6.88 us (6%)
    all_to_all x2, blocking collectives, exchange(): lax.all_to_all(value, 'dp', 0, 0, axis_index_groups=groups, tiled=True)  68.3 us
    all_to_all x1, blocking collectives, body(): lax.all_to_all(copies, 'cols', 0, 0, axis_index_groups=[list(COL_ORDER)],...  16.9 us
    ppermute x1, starting transfers between devices, body(): taken = lax.ppermute(sent, 'dp', [(i, i ^ 1) for i in range(size)])  16 us
    pallas_call x2, Pallas kernels, partial_sums(): pl.pallas_call(functools.partial(partial_kernel, far=far, feats=feats, ot...  4.38 us
    pallas_call x1, Pallas kernels, finish(): pl.pallas_call(functools.partial(final_kernel, feats=weight.shape[0]), ou...  2.4 us
  transfers between devices with their start and end apart: 1, of which 1 were waited for; matrix products, arithmetic and copies ran while one was open for 0% of the time, Pallas kernels for 2%

profile of v3, /device:TPU:1, one launch (start us, length us, event | category | flops | bytes accessed | tf_op | source)
XLA Modules:
  0.0 108.7 jit_solution(14273272895394409396)
XLA Ops:
  0.0 2.2 %partial_other.1 = f32[4,520,128]{2,1,0:T(8,128)S(1)} custom-call(bf16[32,128]{1,0:T(8,128)(2,1)} %bitcast.5, bf16[128,16384]{1,0:T(8,128)(2,1)} %grad_ref.3, f32[1,64]{1,0:T(1,128)} %logit_hbm.3), custom_call_target="tpu_custom_call" | custom-call | tf_op jit(solution)/shard_map/partial_other/pallas_call | solution.py:86
  2.2 16.0 %collective-permute-start = (f32[4,520,128]{2,1,0:T(8,128)S(1)}, f32[4,520,128]{2,1,0:T(8,128)S(1)}, u32[]{:S(2)}, u32[]{:S(2)}) collective-permute-start(f32[4,520,128]{2,1,0:T(8,128)S(1)} %partial_other.1), channel_id=1, source_target_pairs={{0,16},{16,0},{32,48},{48,32},{64,80},{80,64},{96,112},{112,96},{1... | collective-permute-start | bytes 3194888 | tf_op jit(solution)/shard_map/ppermute | solution.py:219
  18.2 2.2 %partial_own.1 = f32[4,520,128]{2,1,0:T(8,128)S(1)} custom-call(bf16[32,128]{1,0:T(8,128)(2,1)} %bitcast.6, bf16[128,16384]{1,0:T(8,128)(2,1)} %grad_ref.3, f32[1,64]{1,0:T(1,128)} %logit_hbm.3), custom_call_target="tpu_custom_call" | custom-call | tf_op jit(solution)/shard_map/partial_own/pallas_call | solution.py:86
  20.4 0.1 collective-permute-done
  20.5 0.5 maximum_select_fusion
  21.1 25.3 %all_to_all.15.in_ref = f32[4,520,128]{2,1,0:T(8,128)S(1)} all-to-all(f32[4,520,128]{2,1,0:T(8,128)S(1)} %maximum_select_fusion), channel_id=1, replica_groups={{96,64,32,0},{224,192,160,128},{352,320,288,256},{480,448,416,384},{608..., dimensions={0} | all-to-all | bytes 2129920 | tf_op jit(solution)/shard_map/all_to_all | solution.py:215
  46.4 0.0 copy-start
  46.4 42.9 %all_to_all.16 = f32[8,1,8320]{2,1,0:T(1,128)S(1)} all-to-all(f32[8,1,8320]{2,1,0:T(1,128)S(1)} %bitcast.4), channel_id=1, replica_groups={{384,256,128,0,896,768,640,512},{400,272,144,16,912,784,656,528},{416,2..., dimensions={0} | all-to-all | bytes 532480 | tf_op jit(solution)/shard_map/all_to_all | solution.py:215
  89.4 0.1 far_sum.1
  89.4 16.9 %all_to_all.17.all_ref = f32[16,64,128]{2,1,0:T(8,128)S(1)} all-to-all(f32[16,64,128]{2,1,0:T(8,128)S(1)} %get-tuple-element.7.own_ref), channel_id=1, replica_groups={{15,14,13,12,11,10,9,8,7,6,5,4,3,2,1,0},{31,30,29,28,27,26,25,24,23,22,..., dimensions={0} | all-to-all | bytes 1048576 | tf_op jit(solution)/shard_map/all_to_all | solution.py:226
  106.3 0.0 copy-done
  106.3 2.4 %finish.1 = f32[32,256]{1,0:T(8,128)} custom-call(f32[16,64,128]{2,1,0:T(8,128)S(1)} %all_to_all.17.all_ref, f32[16,64,128]{2,1,0:T(8,128)S(1)} %get-tuple-element.7.own_ref, f32[8,128]{1,0:T(8,128)S(1)} %get-tuple-element.8.peak_ref, f32[32,256]{1,0:T(8,128)S(1)} %copy-done), custom_call_target="tpu_custom_call" | custom-call | tf_op jit(solution)/shard_map/finish/pallas_call | solution.py:188
  (2 shorter events, 0.1 us)
Async XLA Ops:
  2.2 18.3 %collective-permute-start = (f32[4,520,128]{2,1,0:T(8,128)S(1)}, f32[4,520,128]{2,1,0:T(8,128)S(1)}, u32[]{:S(2)}, u32[]{:S(2)}) collective-permute-start(f32[4,520,128]{2,1,0:T(8,128)S(1)} %partial_other.1), channel_id=1, source_target_pairs={{0,16},{16,0},{32,48},{48,32},{64,80},{80,64},{96,112},{112,96},{1... | collective-permute-start | bytes 3194888 | tf_op jit(solution)/shard_map/ppermute | solution.py:219
  46.4 59.9 %copy-start = (f32[32,256]{1,0:T(8,128)S(1)}, f32[32,256]{1,0:T(8,128)}, u32[]{:S(2)}) copy-start(f32[32,256]{1,0:T(8,128)} %weight_ref.1) | copy-start | bytes 98308

commit v4 on v3

--- a/solution.py
+++ b/solution.py
@@ -15,8 +15,8 @@
 CORES = 2
 NEAR = 4
 GROUPS = 2
-FAR_ORDER = (3, 2, 1, 0, 7, 6, 5, 4)
-NEAR_ORDER = (3, 2, 1, 0)
+FAR_ORDER = (4, 3, 2, 1, 0, 7, 6, 5)
+NEAR_ORDER = (1, 0, 3, 2)
 COL_ORDER = (15, 14, 13, 12, 11, 10, 9, 8, 7, 6, 5, 4, 3, 2, 1, 0)
 
 coef_first = 3.4445

time: 109 us -> 108 us (level)
  blocking collectives: 85.2 us -> 83.5 us
    all_to_all x1, blocking collectives: 16.9 us -> 15.5 us  [body(): lax.all_to_all(copies, 'cols', 0, 0, axis_index_groups=[list(COL_ORDER)],...]
where the time goes in v4:
time: 108 us; the launch traced here: 107 us
  blocking collectives  83.5 us (77%)
  starting transfers between devices  16 us (15%)
  Pallas kernels  6.89 us (6%)
    all_to_all x2, blocking collectives, exchange(): lax.all_to_all(value, 'dp', 0, 0, axis_index_groups=groups, tiled=True)  68 us
    ppermute x1, starting transfers between devices, body(): taken = lax.ppermute(sent, 'dp', [(i, i ^ 1) for i in range(size)])  16 us
    all_to_all x1, blocking collectives, body(): lax.all_to_all(copies, 'cols', 0, 0, axis_index_groups=[list(COL_ORDER)],...  15.5 us
    pallas_call x2, Pallas kernels, partial_sums(): pl.pallas_call(functools.partial(partial_kernel, far=far, feats=feats, ot...  4.38 us
    pallas_call x1, Pallas kernels, finish(): pl.pallas_call(functools.partial(final_kernel, feats=weight.shape[0]), ou...  2.4 us
  transfers between devices with their start and end apart: 1, of which 1 were waited for; matrix products, arithmetic and copies ran while one was open for 0% of the time, Pallas kernels for 2%

profile of v4, /device:TPU:1, one launch (start us, length us, event | category | flops | bytes accessed | tf_op | source)
XLA Modules:
  0.0 107.1 jit_solution(15586221021035631621)
XLA Ops:
  0.0 2.2 %partial_other.1 = f32[4,520,128]{2,1,0:T(8,128)S(1)} custom-call(bf16[32,128]{1,0:T(8,128)(2,1)} %bitcast.5, bf16[128,16384]{1,0:T(8,128)(2,1)} %grad_ref.3, f32[1,64]{1,0:T(1,128)} %logit_hbm.3), custom_call_target="tpu_custom_call" | custom-call | tf_op jit(solution)/shard_map/partial_other/pallas_call | solution.py:86
  2.2 16.0 %collective-permute-start = (f32[4,520,128]{2,1,0:T(8,128)S(1)}, f32[4,520,128]{2,1,0:T(8,128)S(1)}, u32[]{:S(2)}, u32[]{:S(2)}) collective-permute-start(f32[4,520,128]{2,1,0:T(8,128)S(1)} %partial_other.1), channel_id=1, source_target_pairs={{0,16},{16,0},{32,48},{48,32},{64,80},{80,64},{96,112},{112,96},{1... | collective-permute-start | bytes 3194888 | tf_op jit(solution)/shard_map/ppermute | solution.py:219
  18.2 2.2 %partial_own.1 = f32[4,520,128]{2,1,0:T(8,128)S(1)} custom-call(bf16[32,128]{1,0:T(8,128)(2,1)} %bitcast.6, bf16[128,16384]{1,0:T(8,128)(2,1)} %grad_ref.3, f32[1,64]{1,0:T(1,128)} %logit_hbm.3), custom_call_target="tpu_custom_call" | custom-call | tf_op jit(solution)/shard_map/partial_own/pallas_call | solution.py:86
  20.4 0.1 collective-permute-done
  20.5 0.5 maximum_select_fusion
  21.1 26.4 %all_to_all.15.in_ref = f32[4,520,128]{2,1,0:T(8,128)S(1)} all-to-all(f32[4,520,128]{2,1,0:T(8,128)S(1)} %maximum_select_fusion), channel_id=1, replica_groups={{32,0,96,64},{160,128,224,192},{288,256,352,320},{416,384,480,448},{544..., dimensions={0} | all-to-all | bytes 2129920 | tf_op jit(solution)/shard_map/all_to_all | solution.py:215
  47.5 0.0 copy-start
  47.6 41.6 %all_to_all.16 = f32[8,1,8320]{2,1,0:T(1,128)S(1)} all-to-all(f32[8,1,8320]{2,1,0:T(1,128)S(1)} %bitcast.4), channel_id=1, replica_groups={{512,384,256,128,0,896,768,640},{528,400,272,144,16,912,784,656},{544,4..., dimensions={0} | all-to-all | bytes 532480 | tf_op jit(solution)/shard_map/all_to_all | solution.py:215
  89.1 0.1 far_sum.1
  89.2 15.5 %all_to_all.17.all_ref = f32[16,64,128]{2,1,0:T(8,128)S(1)} all-to-all(f32[16,64,128]{2,1,0:T(8,128)S(1)} %get-tuple-element.7.own_ref), channel_id=1, replica_groups={{15,14,13,12,11,10,9,8,7,6,5,4,3,2,1,0},{31,30,29,28,27,26,25,24,23,22,..., dimensions={0} | all-to-all | bytes 1048576 | tf_op jit(solution)/shard_map/all_to_all | solution.py:226
  104.7 0.0 copy-done
  104.7 2.4 %finish.1 = f32[32,256]{1,0:T(8,128)} custom-call(f32[16,64,128]{2,1,0:T(8,128)S(1)} %all_to_all.17.all_ref, f32[16,64,128]{2,1,0:T(8,128)S(1)} %get-tuple-element.7.own_ref, f32[8,128]{1,0:T(8,128)S(1)} %get-tuple-element.8.peak_ref, f32[32,256]{1,0:T(8,128)S(1)} %copy-done), custom_call_target="tpu_custom_call" | custom-call | tf_op jit(solution)/shard_map/finish/pallas_call | solution.py:188
  (2 shorter events, 0.1 us)
Async XLA Ops:
  2.2 18.3 %collective-permute-start = (f32[4,520,128]{2,1,0:T(8,128)S(1)}, f32[4,520,128]{2,1,0:T(8,128)S(1)}, u32[]{:S(2)}, u32[]{:S(2)}) collective-permute-start(f32[4,520,128]{2,1,0:T(8,128)S(1)} %partial_other.1), channel_id=1, source_target_pairs={{0,16},{16,0},{32,48},{48,32},{64,80},{80,64},{96,112},{112,96},{1... | collective-permute-start | bytes 3194888 | tf_op jit(solution)/shard_map/ppermute | solution.py:219
  47.5 57.1 %copy-start = (f32[32,256]{1,0:T(8,128)S(1)}, f32[32,256]{1,0:T(8,128)}, u32[]{:S(2)}) copy-start(f32[32,256]{1,0:T(8,128)} %weight_ref.1) | copy-start | bytes 98308
